TPU v7x, 256 devices: a whole 4x4x8 slice. The times are simulated.
256 devices in a mesh: sector: 128 (over z, y_lo, x, core), blk: 2 (over y_hi).
Axes of the slice: x: 4, y: 4 (y_hi: 2, y_lo: 2; y = y_hi * 2 + y_lo), z: 8, core: 2. Of those that a mesh axis runs over, the one named last changes fastest.
Arguments:
- signal: bfloat16 [4, 4096, 8192], P('blk', 'sector'), may hold values from -6 to 6
- offsets: int32 [4], P('blk'), may hold values from 0 to 4095
- fraction: float32 [4, 8192], P('blk'), may hold values from 0 to 1
- radius: float32 [256], replicated, may hold values from 0.2 to 0.9
- azimuth: float32 [256], replicated, may hold values from -3.140625 to 3.140625
Outputs:
- power: float32 [512, 256], P(('sector', 'blk'))
All inputs are finite; a program needn't handle non-finite values.
Results may differ from a plain program's by a relative error of at most 0.00095.
Values may be sent and summed in bfloat16 or wider, within the bound.
No kernel may reach another device: no remote copies, remote signals or barrier semaphores. Data moves between devices by JAX's collectives and lax.ppermute only.
A program may use at most 64 MiB of HBM per device.

v0:
```python
import math
import jax
import jax.numpy as jnp
from jax import lax
from jax.sharding import PartitionSpec as P

NFFT = 1024
wavenumber = 2.0
height = 0.5


def from_behind(x, axis, by):
    size = lax.axis_size(axis)
    return lax.ppermute(x, axis, [(i, (i + by) % size) for i in range(size)])


def fourier_table(groups):
    half_bins = NFFT // 2
    per_group = half_bins // groups
    sample = lax.iota(jnp.int32, NFFT)[:, None]
    column = lax.iota(jnp.int32, 2 * half_bins)[None, :]
    group = column // (2 * per_group)
    part = column // per_group % 2
    inner = column % per_group
    frequency = group * per_group + inner
    turns = (sample * frequency % NFFT).astype(jnp.float32)
    angle = turns * (2.0 * math.pi / NFFT)
    window = 0.5 - 0.5 * jnp.cos(sample.astype(jnp.float32) * (2.0 * math.pi / NFFT))
    value = jnp.where(part == 0, jnp.cos(angle), -jnp.sin(angle))
    return (value * window / math.sqrt(3.0 * NFFT / 8.0)).astype(jnp.bfloat16)


def distances(radius, azimuth, total_mics):
    turn = lax.iota(jnp.int32, total_mics).astype(jnp.float32) * (2.0 * math.pi / total_mics)
    cycle_cos = jnp.cos(turn)[:, None]
    cycle_sin = jnp.sin(turn)[:, None]
    across = (radius * jnp.cos(azimuth))[None, :]
    along = (radius * jnp.sin(azimuth))[None, :]
    squared = (
        1.0
        + height * height
        + (radius * radius)[None, :]
        - 2.0 * (cycle_cos * across + cycle_sin * along)
    )
    return jnp.sqrt(squared)


def steering(frequency, distance):
    phase = wavenumber * frequency.astype(jnp.float32) * distance
    return jnp.concatenate([jnp.cos(phase), jnp.sin(phase)], 1).astype(jnp.bfloat16)


def interpolate(window_rows, weight):
    lower = window_rows[:, :-1].astype(jnp.float32)
    upper = window_rows[:, 1:].astype(jnp.float32)
    spread_weight = weight[:, None, :]
    return ((1.0 - spread_weight) * lower + spread_weight * upper).astype(jnp.bfloat16)


def segment_spectra(virtual, table):
    blocks, mics, length = virtual.shape
    half = NFFT // 2
    halves = virtual.reshape(blocks, mics, length // half, half)
    upper = jnp.einsum(
        "bmhn,nc->bhcm", halves[:, :, :-1], table[:half], preferred_element_type=jnp.float32
    )
    lower = jnp.einsum(
        "bmhn,nc->bhcm", halves[:, :, 1:], table[half:], preferred_element_type=jnp.float32
    )
    return (upper + lower).astype(jnp.bfloat16)


def band_power(flat, first, count, distance):
    snapshots = flat.shape[0]
    points = distance.shape[1]

    def one_bin(bin_place):
        picked = lax.dynamic_index_in_dim(flat, bin_place, 2, keepdims=False)
        stacked = jnp.concatenate([picked[:, 0], picked[:, 1]], 0)
        steer = steering(first + bin_place, distance)
        product = jnp.dot(stacked, steer, preferred_element_type=jnp.float32)
        along = product[:snapshots, :points] + product[snapshots:, points:]
        across = product[snapshots:, :points] - product[:snapshots, points:]
        return jnp.sum(along * along + across * across, 0)

    return lax.map(one_bin, jnp.arange(count, dtype=jnp.int32))


def local(signal, offsets, fraction, radius, azimuth):
    blocks, mics, length = signal.shape
    sectors = lax.axis_size("sector")
    sector_index = lax.axis_index("sector")
    total_mics = mics * sectors
    hop_count = offsets // mics
    within = offsets % mics
    current = signal
    for place in range((sectors - 1).bit_length()):
        moved = from_behind(current, "sector", -(1 << place))
        chosen = hop_count // (1 << place) % 2 == 1
        current = jnp.where(chosen[:, None, None], moved, current)
    following = from_behind(current, "sector", -1)
    joined = jnp.concatenate([current, following], 1)
    window_rows = jax.vmap(lambda rows, start: lax.dynamic_slice_in_dim(rows, start, mics + 1, 0))(
        joined, within
    )
    virtual = interpolate(window_rows, fraction)
    spectra = segment_spectra(virtual, fourier_table(sectors))
    banded = lax.all_to_all(spectra, "sector", split_axis=2, concat_axis=3, tiled=True)
    segments = banded.shape[1]
    per_sector = banded.shape[2] // 2
    grouped = banded.reshape(blocks, segments, 2, per_sector, total_mics)
    distance = distances(radius, azimuth, total_mics)
    scale = 1.0 / (total_mics * blocks * segments * lax.axis_size("blk"))
    flat = grouped.reshape(blocks * segments, 2, per_sector, total_mics)
    partial_power = band_power(flat, sector_index * per_sector, per_sector, distance) * scale
    return lax.psum_scatter(partial_power, "blk", scatter_dimension=0, tiled=True)


def solution(mesh):
    return jax.shard_map(
        local,
        mesh=mesh,
        in_specs=(P("blk", "sector", None), P("blk"), P("blk", None), P(), P()),
        out_specs=P(("sector", "blk"), None),
        check_vma=False,
    )
```

profile of v0, /device:TPU:24, one launch (start us, length us, event | category | flops | bytes accessed | tf_op | source)
XLA Modules:
  0.0 481.5 jit_solution(11197837299432246893)
XLA Ops:
  0.0 2.4 collective-permute-start
  2.4 0.7 fusion.43
  3.1 11.9 %collective-permute-done = bf16[2,32,8192]{2,1,0:T(8,128)(2,1)S(1)} collective-permute-done((bf16[2,32,8192]{2,1,0:T(8,128)(2,1)}, bf16[2,32,8192]{2,1,0:T(8,128)(2,1)S(1)}, u32[]{:S(2)}, u32[]{:S(2)}) %collective-permute-start) | collective-permute-done | bytes 1048608 | tf_op jit(solution)/shard_map/ppermute | solution.py:14
  15.0 1.4 broadcast_select_fusion
  16.5 0.9 collective-permute-start.1
  17.4 23.5 %collective-permute-done.1 = bf16[2,32,8192]{2,1,0:T(8,128)(2,1)S(1)} collective-permute-done((bf16[2,32,8192]{2,1,0:T(8,128)(2,1)S(1)}, bf16[2,32,8192]{2,1,0:T(8,128)(2,1)S(1)}, u32[]{:S(2)}, u32[]{:S(2)}) %collective-permute-start.1) | collective-permute-done | bytes 1048608 | tf_op jit(solution)/shard_map/ppermute | solution.py:14
  41.4 26.4 %collective-permute-done.2 = bf16[2,32,8192]{2,1,0:T(8,128)(2,1)S(1)} collective-permute-done((bf16[2,32,8192]{2,1,0:T(8,128)(2,1)S(1)}, bf16[2,32,8192]{2,1,0:T(8,128)(2,1)S(1)}, u32[]{:S(2)}, u32[]{:S(2)}) %collective-permute-start.2) | collective-permute-done | bytes 1048608 | tf_op jit(solution)/shard_map/ppermute | solution.py:14
  68.0 1.9 collective-permute-start.3
  69.9 23.5 %collective-permute-done.3 = bf16[2,32,8192]{2,1,0:T(8,128)(2,1)S(1)} collective-permute-done((bf16[2,32,8192]{2,1,0:T(8,128)(2,1)S(1)}, bf16[2,32,8192]{2,1,0:T(8,128)(2,1)S(1)}, u32[]{:S(2)}, u32[]{:S(2)}) %collective-permute-start.3) | collective-permute-done | bytes 1048608 | tf_op jit(solution)/shard_map/ppermute | solution.py:14
  93.5 7.1 %collective-permute-start.4 = (bf16[2,32,8192]{2,1,0:T(8,128)(2,1)S(1)}, bf16[2,32,8192]{2,1,0:T(8,128)(2,1)S(1)}, u32[]{:S(2)}, u32[]{:S(2)}) collective-permute-start(bf16[2,32,8192]{2,1,0:T(8,128)(2,1)S(1)} %broadcast_select_fusion.3), channel_id=1, source_target_pairs={{0,224},{2,226},{4,228},{6,230},{8,232},{10,234},{12,236},{14,238}... | collective-permute-start | bytes 3145736 | tf_op jit(solution)/shard_map/ppermute | solution.py:14
  100.7 21.0 %collective-permute-done.4 = bf16[2,32,8192]{2,1,0:T(8,128)(2,1)S(1)} collective-permute-done((bf16[2,32,8192]{2,1,0:T(8,128)(2,1)S(1)}, bf16[2,32,8192]{2,1,0:T(8,128)(2,1)S(1)}, u32[]{:S(2)}, u32[]{:S(2)}) %collective-permute-start.4) | collective-permute-done | bytes 1048608 | tf_op jit(solution)/shard_map/ppermute | solution.py:14
  121.9 2.3 collective-permute-start.5
  124.2 30.1 %collective-permute-done.5 = bf16[2,32,8192]{2,1,0:T(8,128)(2,1)S(1)} collective-permute-done((bf16[2,32,8192]{2,1,0:T(8,128)(2,1)S(1)}, bf16[2,32,8192]{2,1,0:T(8,128)(2,1)S(1)}, u32[]{:S(2)}, u32[]{:S(2)}) %collective-permute-start.5) | collective-permute-done | bytes 1048608 | tf_op jit(solution)/shard_map/ppermute | solution.py:14
  154.4 1.8 collective-permute-start.6
  156.3 46.5 %collective-permute-done.6 = bf16[2,32,8192]{2,1,0:T(8,128)(2,1)S(1)} collective-permute-done((bf16[2,32,8192]{2,1,0:T(8,128)(2,1)S(1)}, bf16[2,32,8192]{2,1,0:T(8,128)(2,1)S(1)}, u32[]{:S(2)}, u32[]{:S(2)}) %collective-permute-start.6) | collective-permute-done | bytes 1048608 | tf_op jit(solution)/shard_map/ppermute | solution.py:14
  202.9 10.8 %collective-permute-start.7 = (bf16[2,32,8192]{2,1,0:T(8,128)(2,1)S(1)}, bf16[2,32,8192]{2,1,0:T(8,128)(2,1)}, u32[]{:S(2)}, u32[]{:S(2)}) collective-permute-start(bf16[2,32,8192]{2,1,0:T(8,128)(2,1)S(1)} %broadcast_select_fusion.6), channel_id=1, source_target_pairs={{0,254},{2,0},{4,2},{6,4},{8,6},{10,8},{12,10},{14,12},{16,14},{18... | collective-permute-start | bytes 3145736 | tf_op jit(solution)/shard_map/ppermute | solution.py:14
  213.9 18.0 %multiply_convert_fusion = bf16[1024,1024]{1,0:T(8,128)(2,1)} fusion(f32[1024]{0:T(1024)S(1)} %multiply_subtract_fusion, s32[1024]{0:T(1024)S(1)} %fusion.40, pred[1024]{0:T(1024)(128)(4,1)S(1)} %fusion.37), kind=kLoop, calls=%fused_computation.32 | loop fusion | flops 19922944 | bytes 2106368 | tf_op jit(solution)/shard_map/convert_element_type | solution.py:30
  232.0 1.4 pad_maximum_fusion
  233.3 5.4 %while.12 = (s32[]{:T(128)}, bf16[2,64,8192]{2,1,0:T(8,128)(2,1)S(1)}, s32[2,3]{1,0:T(2,128)S(1)}, bf16[2,33,8192]{2,1,0:T(8,128)(2,1)}, s32[]{:T(128)}) while((s32[]{:T(128)}, bf16[2,64,8192]{2,1,0:T(8,128)(2,1)S(1)}, s32[2,3]{1,0:T(2,128)S(1)}, bf16[2,33,8192]{2,1,0:T(8,128)(2,1)}, s32[]{:T(128)}) %tuple.63), condition=%wide.while_cond, body=%wide.while_body.sunk | while | flops 2 | bytes 1197673 | solution.py:103
  233.9 2.1 dynamic-slice_dynamic-update-slice_fusion.2
  236.6 2.1 dynamic-slice_dynamic-update-slice_fusion.2
  238.7 2.3 add_convert_fusion.1
  241.9 1.4 fusion.25
  243.3 1.5 fusion.24
  244.7 12.1 %copy.31 = bf16[2,15,1024,32]{3,0,1,2:T(2,128)(2,1)} copy(bf16[2,15,1024,32]{2,3,1,0:T(8,128)(2,1)S(1)} %fusion.24) | data formatting | bytes 3932160 | tf_op jit(solution)/shard_map/convert_element_type | solution.py:70
  256.8 16.9 %reshape.173 = bf16[128,2,3840]{2,1,0:T(2,128)(2,1)} reshape(bf16[1024,15,2,32]{3,2,1,0:T(2,128)(2,1)} %bitcast.50) | data formatting | bytes 3932160
  273.7 22.3 %all-to-all-start = ((bf16[128,2,3840]{2,1,0:T(2,128)(2,1)}), bf16[128,2,3840]{2,1,0:T(2,128)(2,1)S(1)}, u32[]{:S(2)}, u32[]{:S(2)}) async-start(bf16[128,2,3840]{2,1,0:T(2,128)(2,1)} %reshape.173), calls=%async_computation | async-start | bytes 3932160 | tf_op jit(solution)/shard_map/all_to_all | solution.py:108
  297.4 47.4 %all-to-all-done = bf16[128,2,3840]{2,1,0:T(2,128)(2,1)S(1)} async-done(((bf16[128,2,3840]{2,1,0:T(2,128)(2,1)}), bf16[128,2,3840]{2,1,0:T(2,128)(2,1)S(1)}, u32[]{:S(2)}, u32[]{:S(2)}) %all-to-all-start) | async-done | bytes 1966112 | tf_op jit(solution)/shard_map/all_to_all | solution.py:108
  344.9 6.6 %reshape.174 = bf16[1024,15,2,32]{3,2,1,0:T(2,128)(2,1)} reshape(bf16[128,2,3840]{2,1,0:T(2,128)(2,1)S(1)} %all-to-all-done) | data formatting | bytes 3932160
  351.4 5.0 %copy.49 = bf16[2,15,1024,32]{3,2,1,0:T(8,128)(2,1)S(1)} copy(bf16[2,15,1024,32]{3,0,1,2:T(2,128)(2,1)} %bitcast.51) | data formatting | bytes 3932160 | tf_op jit(solution)/shard_map/all_to_all | solution.py:108
  356.4 5.4 %copy.33 = bf16[2,15,8,128,32]{4,3,2,1,0:T(8,128)(2,1)} copy(bf16[2,15,8,128,32]{4,2,3,1,0:T(8,128)(2,1)S(1)} %bitcast.52) | data formatting | bytes 3932160 | tf_op jit(solution)/shard_map/all_to_all | solution.py:108
  361.9 11.3 %reshape_reshape.3 = bf16[30,2,4,4096]{3,2,1,0:T(4,128)(2,1)} reshape(bf16[2,15,8,128,32]{4,3,2,1,0:T(8,128)(2,1)} %copy.33) | data formatting | bytes 3932160 | tf_op jit(solution)/shard_map/reshape;reshape | solution.py:114
  373.2 3.6 copy.34
  376.8 97.6 %while.13 = (s32[]{:T(128)}, f32[4,256]{1,0:T(4,128)S(1)}, s32[4]{0:T(128)S(1)}, bf16[30,2,4,4096]{3,1,0,2:T(2,128)(2,1)S(1)}, s32[]{:T(128)}, /*index=5*/f32[25...) while((s32[]{:T(128)}, f32[4,256]{1,0:T(4,128)S(1)}, ...), condition=%wide.region_2.3_spmd.clone, body=%wide.region_0.2_spmd.clone.sunk | while | flops 269464320 | bytes 12114143 | solution.py:86
  379.7 1.1 fusion.71
  382.0 18.4 %fusion.70 = (bf16[4096,256]{1,0:T(8,128)(2,1)S(1)}, bf16[4096,256]{1,0:T(8,128)(2,1)S(1)}) fusion(f32[256]{0:T(256)S(1)} %get-tuple-element.336, f32[4096]{0:T(1024)S(1)} %get-tuple-element.337, f32[256]{0:T(256)S(1)} %get-tuple-element.334, f32[4096]{0:T(1024)S(1)} %get-tuple-element.335, f32[256]{0:T(256)S(1)} %get-tuple-element.338, f32[]{:T(128)S(6)} %mul.373), kind=kLoop, calls=%fused_computation.10.clone.1 | loop fusion | flops 8388608 | bytes 4230148 | tf_op jit(solution)/shard_map/convert
  400.4 0.7 fusion.72
  401.2 0.6 dynamic_slice.14
  404.1 1.1 fusion.71
  406.4 18.4 %fusion.70 = (bf16[4096,256]{1,0:T(8,128)(2,1)S(1)}, bf16[4096,256]{1,0:T(8,128)(2,1)S(1)}) fusion(f32[256]{0:T(256)S(1)} %get-tuple-element.336, f32[4096]{0:T(1024)S(1)} %get-tuple-element.337, f32[256]{0:T(256)S(1)} %get-tuple-element.334, f32[4096]{0:T(1024)S(1)} %get-tuple-element.335, f32[256]{0:T(256)S(1)} %get-tuple-element.338, f32[]{:T(128)S(6)} %mul.373), kind=kLoop, calls=%fused_computation.10.clone.1 | loop fusion | flops 8388608 | bytes 4230148 | tf_op jit(solution)/shard_map/convert
  424.8 0.7 fusion.72
  428.5 1.1 fusion.71
  430.8 18.4 %fusion.70 = (bf16[4096,256]{1,0:T(8,128)(2,1)S(1)}, bf16[4096,256]{1,0:T(8,128)(2,1)S(1)}) fusion(f32[256]{0:T(256)S(1)} %get-tuple-element.336, f32[4096]{0:T(1024)S(1)} %get-tuple-element.337, f32[256]{0:T(256)S(1)} %get-tuple-element.334, f32[4096]{0:T(1024)S(1)} %get-tuple-element.335, f32[256]{0:T(256)S(1)} %get-tuple-element.338, f32[]{:T(128)S(6)} %mul.373), kind=kLoop, calls=%fused_computation.10.clone.1 | loop fusion | flops 8388608 | bytes 4230148 | tf_op jit(solution)/shard_map/convert
  449.2 0.7 fusion.72
  452.9 1.1 fusion.71
  455.2 18.4 %fusion.70 = (bf16[4096,256]{1,0:T(8,128)(2,1)S(1)}, bf16[4096,256]{1,0:T(8,128)(2,1)S(1)}) fusion(f32[256]{0:T(256)S(1)} %get-tuple-element.336, f32[4096]{0:T(1024)S(1)} %get-tuple-element.337, f32[256]{0:T(256)S(1)} %get-tuple-element.334, f32[4096]{0:T(1024)S(1)} %get-tuple-element.335, f32[256]{0:T(256)S(1)} %get-tuple-element.338, f32[]{:T(128)S(6)} %mul.373), kind=kLoop, calls=%fused_computation.10.clone.1 | loop fusion | flops 8388608 | bytes 4230148 | tf_op jit(solution)/shard_map/convert
  473.6 0.7 fusion.72
  474.4 6.4 %all-reduce.1 = f32[4,256]{1,0:T(4,128)S(1)} all-reduce(f32[4,256]{1,0:T(4,128)S(1)} %broadcast_multiply_fusion), channel_id=2, replica_groups=mesh['sector'=128,'blk'=2] {'blk'}, use_global_device_ids=true, to_apply=%region_3.4.clone | all-reduce | flops 1024 | bytes 8192
  (62 shorter events, 10.8 us)
Async XLA Ops:
  0.0 15.0 %collective-permute-start = (bf16[2,32,8192]{2,1,0:T(8,128)(2,1)}, bf16[2,32,8192]{2,1,0:T(8,128)(2,1)S(1)}, u32[]{:S(2)}, u32[]{:S(2)}) collective-permute-start(bf16[2,32,8192]{2,1,0:T(8,128)(2,1)} %param.7), channel_id=1, source_target_pairs={{0,254},{2,0},{4,2},{6,4},{8,6},{10,8},{12,10},{14,12},{16,14},{18... | collective-permute-start | bytes 3145736 | tf_op jit(solution)/shard_map/ppermute | solution.py:14
  16.5 24.4 %collective-permute-start.1 = (bf16[2,32,8192]{2,1,0:T(8,128)(2,1)S(1)}, bf16[2,32,8192]{2,1,0:T(8,128)(2,1)S(1)}, u32[]{:S(2)}, u32[]{:S(2)}) collective-permute-start(bf16[2,32,8192]{2,1,0:T(8,128)(2,1)S(1)} %broadcast_select_fusion), channel_id=1, source_target_pairs={{0,252},{2,254},{4,0},{6,2},{8,4},{10,6},{12,8},{14,10},{16,12},{1... | collective-permute-start | bytes 3145736 | tf_op jit(solution)/shard_map/ppermute | solution.py:14
  41.1 26.8 %collective-permute-start.2 = (bf16[2,32,8192]{2,1,0:T(8,128)(2,1)S(1)}, bf16[2,32,8192]{2,1,0:T(8,128)(2,1)S(1)}, u32[]{:S(2)}, u32[]{:S(2)}) collective-permute-start(bf16[2,32,8192]{2,1,0:T(8,128)(2,1)S(1)} %broadcast_select_fusion.1), channel_id=1, source_target_pairs={{0,248},{2,250},{4,252},{6,254},{8,0},{10,2},{12,4},{14,6},{16,8},... | collective-permute-start | bytes 3145736 | tf_op jit(solution)/shard_map/ppermute | solution.py:14
  67.9 56.3 %copy-start.3 = (s32[2]{0:T(128)S(1)}, s32[2]{0:T(128)}, u32[]{:S(2)}) copy-start(s32[2]{0:T(128)} %param.8) | copy-start | bytes 28
  68.0 25.3 %collective-permute-start.3 = (bf16[2,32,8192]{2,1,0:T(8,128)(2,1)S(1)}, bf16[2,32,8192]{2,1,0:T(8,128)(2,1)S(1)}, u32[]{:S(2)}, u32[]{:S(2)}) collective-permute-start(bf16[2,32,8192]{2,1,0:T(8,128)(2,1)S(1)} %broadcast_select_fusion.2), channel_id=1, source_target_pairs={{0,240},{2,242},{4,244},{6,246},{8,248},{10,250},{12,252},{14,254}... | collective-permute-start | bytes 3145736 | tf_op jit(solution)/shard_map/ppermute | solution.py:14
  93.4 62.9 %copy-start = (f32[2,8192]{1,0:T(2,128)S(1)}, f32[2,8192]{1,0:T(2,128)}, u32[]{:S(2)}) copy-start(f32[2,8192]{1,0:T(2,128)} %param.9) | copy-start | bytes 196612
  93.5 28.2 %collective-permute-start.4 = (bf16[2,32,8192]{2,1,0:T(8,128)(2,1)S(1)}, bf16[2,32,8192]{2,1,0:T(8,128)(2,1)S(1)}, u32[]{:S(2)}, u32[]{:S(2)}) collective-permute-start(bf16[2,32,8192]{2,1,0:T(8,128)(2,1)S(1)} %broadcast_select_fusion.3), channel_id=1, source_target_pairs={{0,224},{2,226},{4,228},{6,230},{8,232},{10,234},{12,236},{14,238}... | collective-permute-start | bytes 3145736 | tf_op jit(solution)/shard_map/ppermute | solution.py:14
  121.9 32.4 %collective-permute-start.5 = (bf16[2,32,8192]{2,1,0:T(8,128)(2,1)S(1)}, bf16[2,32,8192]{2,1,0:T(8,128)(2,1)S(1)}, u32[]{:S(2)}, u32[]{:S(2)}) collective-permute-start(bf16[2,32,8192]{2,1,0:T(8,128)(2,1)S(1)} %broadcast_select_fusion.4), channel_id=1, source_target_pairs={{0,192},{2,194},{4,196},{6,198},{8,200},{10,202},{12,204},{14,206}... | collective-permute-start | bytes 3145736 | tf_op jit(solution)/shard_map/ppermute | solution.py:14
  154.4 48.4 %collective-permute-start.6 = (bf16[2,32,8192]{2,1,0:T(8,128)(2,1)S(1)}, bf16[2,32,8192]{2,1,0:T(8,128)(2,1)S(1)}, u32[]{:S(2)}, u32[]{:S(2)}) collective-permute-start(bf16[2,32,8192]{2,1,0:T(8,128)(2,1)S(1)} %broadcast_select_fusion.5), channel_id=1, source_target_pairs={{0,128},{2,130},{4,132},{6,134},{8,136},{10,138},{12,140},{14,142}... | collective-permute-start | bytes 3145736 | tf_op jit(solution)/shard_map/ppermute | solution.py:14
  202.9 29.0 %collective-permute-start.7 = (bf16[2,32,8192]{2,1,0:T(8,128)(2,1)S(1)}, bf16[2,32,8192]{2,1,0:T(8,128)(2,1)}, u32[]{:S(2)}, u32[]{:S(2)}) collective-permute-start(bf16[2,32,8192]{2,1,0:T(8,128)(2,1)S(1)} %broadcast_select_fusion.6), channel_id=1, source_target_pairs={{0,254},{2,0},{4,2},{6,4},{8,6},{10,8},{12,10},{14,12},{16,14},{18... | collective-permute-start | bytes 3145736 | tf_op jit(solution)/shard_map/ppermute | solution.py:14
  238.7 3.2 copy-start.5
  256.8 39.2 %copy-start.4 = (u32[256]{0:T(256)S(1)}, u32[256]{0:T(256)}, u32[]{:S(2)}) copy-start(u32[256]{0:T(256)} %constant.255) | copy-start | bytes 3076
  256.8 40.5 %copy-start.1 = (f32[256]{0:T(256)S(1)}, f32[256]{0:T(256)}, u32[]{:S(2)}) copy-start(f32[256]{0:T(256)} %param.10) | copy-start | bytes 3076
  256.8 40.5 %copy-start.2 = (f32[256]{0:T(256)S(1)}, f32[256]{0:T(256)}, u32[]{:S(2)}) copy-start(f32[256]{0:T(256)} %param.11) | copy-start | bytes 3076
  273.7 71.1 %all-to-all-start = ((bf16[128,2,3840]{2,1,0:T(2,128)(2,1)}), bf16[128,2,3840]{2,1,0:T(2,128)(2,1)S(1)}, u32[]{:S(2)}, u32[]{:S(2)}) async-start(bf16[128,2,3840]{2,1,0:T(2,128)(2,1)} %reshape.173), calls=%async_computation | async-start | bytes 3932160 | tf_op jit(solution)/shard_map/all_to_all | solution.py:108
where the time goes:
time: 482 us; the launch traced here: 481 us
  waiting for transfers between devices  230 us (48%)
  other arithmetic  98.7 us (20%)
  local copies, waits for them, and re-layouts  79.3 us (16%)
  starting transfers between devices  49.8 us (10%)
  loops' own time  10.3 us (2%)
  blocking collectives  6.45 us (1%)
  matrix products  5.78 us (1%)
    ppermute x8, waiting for transfers between devices, from_behind(): return lax.ppermute(x, axis, [(i, (i + by) % size) for i in range(size)])  183 us
    another operation x4, other arithmetic  73.4 us
    all_to_all x1, waiting for transfers between devices, local(): lax.all_to_all(spectra, 'sector', split_axis=2, concat_axis=3, tiled=True)  47.4 us
    unnamed x20, local copies, waits for them, and re-layouts  28.7 us
    ppermute x8, starting transfers between devices, from_behind(): return lax.ppermute(x, axis, [(i, (i + by) % size) for i in range(size)])  27.6 us
    all_to_all x1, starting transfers between devices, local(): lax.all_to_all(spectra, 'sector', split_axis=2, concat_axis=3, tiled=True)  22.3 us
    convert_element_type x1, other arithmetic, fourier_table(): return (value * window / math.sqrt(3.0 * NFFT / 8.0)).astype(jnp.bfloat16)  18 us
    convert_element_type x1, local copies, waits for them, and re-layouts, segment_spectra(): return (upper + lower).astype(jnp.bfloat16)  12.1 us
  transfers between devices with their start and end apart: 9, of which 8 were waited for; matrix products, arithmetic and copies ran while one was open for 4% of the time, Pallas kernels for 0%

commit v1 on v0

--- a/solution.py
+++ b/solution.py
@@ -105,7 +105,12 @@
     )
     virtual = interpolate(window_rows, fraction)
     spectra = segment_spectra(virtual, fourier_table(sectors))
-    banded = lax.all_to_all(spectra, "sector", split_axis=2, concat_axis=3, tiled=True)
+    banded = jnp.concatenate(
+        lax.all_to_all(
+            jnp.stack(jnp.split(spectra, lax.axis_size("sector"), axis=2)), "sector", 0, 0
+        ),
+        axis=3,
+    )
     segments = banded.shape[1]
     per_sector = banded.shape[2] // 2
     grouped = banded.reshape(blocks, segments, 2, per_sector, total_mics)

time: 482 us -> 608 us (1.26); the launches traced: 481 us -> 599 us
  local copies, waits for them, and re-layouts: 79.3 us -> 193 us
    unnamed x20 -> x143, local copies, waits for them, and re-layouts: 28.7 us -> 130 us
    another operation x0 -> x2, local copies, waits for them, and re-layouts: none -> 26.2 us  [local(): jnp.stack(jnp.split(spectra, lax.axis_size('sector'), axis=2))]
    convert_element_type x1 -> x0, local copies, waits for them, and re-layouts: 12.1 us -> none  [segment_spectra(): return (upper + lower).astype(jnp.bfloat16)]
    all_to_all x2 -> x0, local copies, waits for them, and re-layouts: 10.4 us -> none  [local(): lax.all_to_all(spectra, 'sector', split_axis=2, concat_axis=3, tiled=True)]
    reshape x0 -> x1, local copies, waits for them, and re-layouts: none -> 8.62 us  [local(): jnp.concatenate(lax.all_to_all(jnp.stack(jnp.split(spectra, lax.axis_size...]
where the time goes in v1:
time: 608 us; the launch traced here: 599 us
  waiting for transfers between devices  229 us (38%)
  local copies, waits for them, and re-layouts  193 us (32%)
  other arithmetic  100 us (16%)
  starting transfers between devices  49.6 us (8%)
  loops' own time  11.8 us (2%)
  matrix products  8.23 us (1%)
  blocking collectives  6.45 us (1%)
    ppermute x8, waiting for transfers between devices, from_behind(): return lax.ppermute(x, axis, [(i, (i + by) % size) for i in range(size)])  181 us
    unnamed x143, local copies, waits for them, and re-layouts  130 us
    another operation x4, other arithmetic  73.4 us
    all_to_all x1, waiting for transfers between devices, local(): lax.all_to_all(jnp.stack(jnp.split(spectra, lax.axis_size('sector'), axis...  47.4 us
    ppermute x8, starting transfers between devices, from_behind(): return lax.ppermute(x, axis, [(i, (i + by) % size) for i in range(size)])  27.4 us
    another operation x2, local copies, waits for them, and re-layouts, local(): jnp.stack(jnp.split(spectra, lax.axis_size('sector'), axis=2))  26.2 us
    all_to_all x1, starting transfers between devices, local(): lax.all_to_all(jnp.stack(jnp.split(spectra, lax.axis_size('sector'), axis...  22.3 us
    convert_element_type x1, other arithmetic, fourier_table(): return (value * window / math.sqrt(3.0 * NFFT / 8.0)).astype(jnp.bfloat16)  18.1 us
  transfers between devices with their start and end apart: 9, of which 8 were waited for; matrix products, arithmetic and copies ran while one was open for 4% of the time, Pallas kernels for 0%

profile of v1, /device:TPU:24, one launch (start us, length us, event | category | flops | bytes accessed | tf_op | source)
XLA Modules:
  0.0 599.4 jit_solution(9747245441512234913)
XLA Ops:
  0.0 2.4 collective-permute-start
  3.1 11.9 %collective-permute-done = bf16[2,32,8192]{2,1,0:T(8,128)(2,1)S(1)} collective-permute-done((bf16[2,32,8192]{2,1,0:T(8,128)(2,1)}, bf16[2,32,8192]{2,1,0:T(8,128)(2,1)S(1)}, u32[]{:S(2)}, u32[]{:S(2)}) %collective-permute-start) | collective-permute-done | bytes 1048608 | tf_op jit(solution)/shard_map/ppermute | solution.py:14
  15.0 1.4 broadcast_select_fusion
  16.5 0.9 collective-permute-start.1
  17.4 23.5 %collective-permute-done.1 = bf16[2,32,8192]{2,1,0:T(8,128)(2,1)S(1)} collective-permute-done((bf16[2,32,8192]{2,1,0:T(8,128)(2,1)S(1)}, bf16[2,32,8192]{2,1,0:T(8,128)(2,1)S(1)}, u32[]{:S(2)}, u32[]{:S(2)}) %collective-permute-start.1) | collective-permute-done | bytes 1048608 | tf_op jit(solution)/shard_map/ppermute | solution.py:14
  41.4 26.4 %collective-permute-done.2 = bf16[2,32,8192]{2,1,0:T(8,128)(2,1)S(1)} collective-permute-done((bf16[2,32,8192]{2,1,0:T(8,128)(2,1)S(1)}, bf16[2,32,8192]{2,1,0:T(8,128)(2,1)S(1)}, u32[]{:S(2)}, u32[]{:S(2)}) %collective-permute-start.2) | collective-permute-done | bytes 1048608 | tf_op jit(solution)/shard_map/ppermute | solution.py:14
  68.0 1.9 collective-permute-start.3
  69.9 23.5 %collective-permute-done.3 = bf16[2,32,8192]{2,1,0:T(8,128)(2,1)S(1)} collective-permute-done((bf16[2,32,8192]{2,1,0:T(8,128)(2,1)S(1)}, bf16[2,32,8192]{2,1,0:T(8,128)(2,1)S(1)}, u32[]{:S(2)}, u32[]{:S(2)}) %collective-permute-start.3) | collective-permute-done | bytes 1048608 | tf_op jit(solution)/shard_map/ppermute | solution.py:14
  93.5 7.1 %collective-permute-start.4 = (bf16[2,32,8192]{2,1,0:T(8,128)(2,1)S(1)}, bf16[2,32,8192]{2,1,0:T(8,128)(2,1)S(1)}, u32[]{:S(2)}, u32[]{:S(2)}) collective-permute-start(bf16[2,32,8192]{2,1,0:T(8,128)(2,1)S(1)} %broadcast_select_fusion.3), channel_id=1, source_target_pairs={{0,224},{2,226},{4,228},{6,230},{8,232},{10,234},{12,236},{14,238}... | collective-permute-start | bytes 3145736 | tf_op jit(solution)/shard_map/ppermute | solution.py:14
  100.7 21.0 %collective-permute-done.4 = bf16[2,32,8192]{2,1,0:T(8,128)(2,1)S(1)} collective-permute-done((bf16[2,32,8192]{2,1,0:T(8,128)(2,1)S(1)}, bf16[2,32,8192]{2,1,0:T(8,128)(2,1)S(1)}, u32[]{:S(2)}, u32[]{:S(2)}) %collective-permute-start.4) | collective-permute-done | bytes 1048608 | tf_op jit(solution)/shard_map/ppermute | solution.py:14
  121.9 2.3 collective-permute-start.5
  124.8 29.4 %collective-permute-done.5 = bf16[2,32,8192]{2,1,0:T(8,128)(2,1)S(1)} collective-permute-done((bf16[2,32,8192]{2,1,0:T(8,128)(2,1)S(1)}, bf16[2,32,8192]{2,1,0:T(8,128)(2,1)S(1)}, u32[]{:S(2)}, u32[]{:S(2)}) %collective-permute-start.5) | collective-permute-done | bytes 1048608 | tf_op jit(solution)/shard_map/ppermute | solution.py:14
  154.4 1.8 collective-permute-start.6
  156.2 0.9 broadcast_subtract_fusion
  157.1 45.7 %collective-permute-done.6 = bf16[2,32,8192]{2,1,0:T(8,128)(2,1)S(1)} collective-permute-done((bf16[2,32,8192]{2,1,0:T(8,128)(2,1)S(1)}, bf16[2,32,8192]{2,1,0:T(8,128)(2,1)S(1)}, u32[]{:S(2)}, u32[]{:S(2)}) %collective-permute-start.6) | collective-permute-done | bytes 1048608 | tf_op jit(solution)/shard_map/ppermute | solution.py:14
  202.9 10.6 %collective-permute-start.7 = (bf16[2,32,8192]{2,1,0:T(8,128)(2,1)S(1)}, bf16[2,32,8192]{2,1,0:T(8,128)(2,1)}, u32[]{:S(2)}, u32[]{:S(2)}) collective-permute-start(bf16[2,32,8192]{2,1,0:T(8,128)(2,1)S(1)} %broadcast_select_fusion.6), channel_id=1, source_target_pairs={{0,254},{2,0},{4,2},{6,4},{8,6},{10,8},{12,10},{14,12},{16,14},{18... | collective-permute-start | bytes 3145736 | tf_op jit(solution)/shard_map/ppermute | solution.py:14
  213.7 18.1 %multiply_convert_fusion = bf16[1024,1024]{1,0:T(8,128)(2,1)} fusion(f32[1024]{0:T(1024)S(1)} %multiply_subtract_fusion, s32[1024]{0:T(1024)S(1)} %fusion.40, pred[1024]{0:T(1024)(128)(4,1)S(1)} %fusion.37), kind=kLoop, calls=%fused_computation.31 | loop fusion | flops 19922944 | bytes 2106368 | tf_op jit(solution)/shard_map/convert_element_type | solution.py:30
  231.8 1.4 pad_maximum_fusion
  233.2 6.4 %while.12 = (s32[]{:T(128)}, bf16[2,64,8192]{2,1,0:T(8,128)(2,1)S(1)}, s32[2,3]{1,0:T(2,128)S(1)}, bf16[2,33,8192]{2,1,0:T(8,128)(2,1)}, s32[]{:T(128)}) while((s32[]{:T(128)}, bf16[2,64,8192]{2,1,0:T(8,128)(2,1)S(1)}, s32[2,3]{1,0:T(2,128)S(1)}, bf16[2,33,8192]{2,1,0:T(8,128)(2,1)}, s32[]{:T(128)}) %tuple.63), condition=%wide.while_cond, body=%wide.while_body.sunk | while | flops 2 | bytes 1197673 | solution.py:103
  233.8 2.3 dynamic-slice_dynamic-update-slice_fusion.2
  236.8 2.3 dynamic-slice_dynamic-update-slice_fusion.2
  239.6 2.2 add_convert_fusion.1
  242.6 2.6 fusion.25
  245.2 2.7 fusion.24
  277.1 0.9 constant_dynamic-update-slice_fusion.92
  277.9 0.9 constant_dynamic-update-slice_fusion.91
  297.2 1.0 constant_dynamic-update-slice_fusion.68
  314.0 0.9 constant_dynamic-update-slice_fusion.48
  322.3 0.9 constant_dynamic-update-slice_fusion.38
  333.1 0.9 constant_dynamic-update-slice_fusion.25
  354.9 25.3 %copy.155 = bf16[128,2,15,8,32]{4,3,2,1,0:T(8,128)(2,1)} copy(bf16[128,2,15,8,32]{3,4,2,1,0:T(8,128)(2,1)} %constant_dynamic-update-slice_fusion) | data formatting | bytes 3932160 | tf_op jit(solution)/shard_map/stack | solution.py:110
  380.2 11.7 %reshape.176 = bf16[128,2,3840]{2,1,0:T(2,128)(2,1)} reshape(bf16[128,2,15,8,32]{4,3,2,1,0:T(8,128)(2,1)} %copy.155) | data formatting | bytes 3932160
  391.9 22.3 %all-to-all-start = ((bf16[128,2,3840]{2,1,0:T(2,128)(2,1)}), bf16[128,2,3840]{2,1,0:T(2,128)(2,1)S(1)}, u32[]{:S(2)}, u32[]{:S(2)}) async-start(bf16[128,2,3840]{2,1,0:T(2,128)(2,1)} %reshape.176), calls=%async_computation | async-start | bytes 3932160 | tf_op jit(solution)/shard_map/all_to_all | solution.py:109
  415.7 47.4 %all-to-all-done = bf16[128,2,3840]{2,1,0:T(2,128)(2,1)S(1)} async-done(((bf16[128,2,3840]{2,1,0:T(2,128)(2,1)}), bf16[128,2,3840]{2,1,0:T(2,128)(2,1)S(1)}, u32[]{:S(2)}, u32[]{:S(2)}) %all-to-all-start) | async-done | bytes 1966112 | tf_op jit(solution)/shard_map/all_to_all | solution.py:109
  463.0 6.7 %reshape.177 = bf16[128,2,15,8,32]{4,3,2,1,0:T(8,128)(2,1)} reshape(bf16[128,2,3840]{2,1,0:T(2,128)(2,1)S(1)} %all-to-all-done) | data formatting | bytes 3932160
  469.7 8.6 %copy.156 = bf16[2,15,8,128,32]{4,3,2,1,0:T(8,128)(2,1)} copy(bf16[2,15,8,128,32]{4,2,1,0,3:T(8,128)(2,1)} %bitcast.556) | data formatting | bytes 3932160 | tf_op jit(solution)/shard_map/reshape | solution.py:108
  478.3 11.3 %reshape_reshape_reshape.3 = bf16[30,2,4,4096]{3,2,1,0:T(4,128)(2,1)} reshape(bf16[2,15,8,128,32]{4,3,2,1,0:T(8,128)(2,1)} %copy.156) | data formatting | bytes 3932160 | tf_op jit(solution)/shard_map/reshape;reshape;reshape | solution.py:119
  489.7 3.6 copy.157
  493.3 98.9 %while.13 = (s32[]{:T(128)}, f32[4,256]{1,0:T(4,128)S(1)}, s32[4]{0:T(128)S(1)}, bf16[30,2,4,4096]{3,1,0,2:T(2,128)(2,1)S(1)}, s32[]{:T(128)}, /*index=5*/f32[25...) while((s32[]{:T(128)}, f32[4,256]{1,0:T(4,128)S(1)}, ...), condition=%wide.region_2.3_spmd.clone, body=%wide.region_0.2_spmd.clone.sunk | while | flops 269464320 | bytes 12114143 | solution.py:86
  496.4 1.1 fusion.71
  498.8 18.4 %fusion.70 = (bf16[4096,256]{1,0:T(8,128)(2,1)S(1)}, bf16[4096,256]{1,0:T(8,128)(2,1)S(1)}) fusion(f32[256]{0:T(256)S(1)} %get-tuple-element.336, f32[4096]{0:T(1024)S(1)} %get-tuple-element.337, f32[256]{0:T(256)S(1)} %get-tuple-element.334, f32[4096]{0:T(1024)S(1)} %get-tuple-element.335, f32[256]{0:T(256)S(1)} %get-tuple-element.338, f32[]{:T(128)S(6)} %mul.373), kind=kLoop, calls=%fused_computation.10.clone.1 | loop fusion | flops 8388608 | bytes 4230148 | tf_op jit(solution)/shard_map/convert
  521.2 1.1 fusion.71
  523.5 18.4 %fusion.70 = (bf16[4096,256]{1,0:T(8,128)(2,1)S(1)}, bf16[4096,256]{1,0:T(8,128)(2,1)S(1)}) fusion(f32[256]{0:T(256)S(1)} %get-tuple-element.336, f32[4096]{0:T(1024)S(1)} %get-tuple-element.337, f32[256]{0:T(256)S(1)} %get-tuple-element.334, f32[4096]{0:T(1024)S(1)} %get-tuple-element.335, f32[256]{0:T(256)S(1)} %get-tuple-element.338, f32[]{:T(128)S(6)} %mul.373), kind=kLoop, calls=%fused_computation.10.clone.1 | loop fusion | flops 8388608 | bytes 4230148 | tf_op jit(solution)/shard_map/convert
  545.9 1.1 fusion.71
  548.3 18.4 %fusion.70 = (bf16[4096,256]{1,0:T(8,128)(2,1)S(1)}, bf16[4096,256]{1,0:T(8,128)(2,1)S(1)}) fusion(f32[256]{0:T(256)S(1)} %get-tuple-element.336, f32[4096]{0:T(1024)S(1)} %get-tuple-element.337, f32[256]{0:T(256)S(1)} %get-tuple-element.334, f32[4096]{0:T(1024)S(1)} %get-tuple-element.335, f32[256]{0:T(256)S(1)} %get-tuple-element.338, f32[]{:T(128)S(6)} %mul.373), kind=kLoop, calls=%fused_computation.10.clone.1 | loop fusion | flops 8388608 | bytes 4230148 | tf_op jit(solution)/shard_map/convert
  570.6 1.1 fusion.71
  573.0 18.4 %fusion.70 = (bf16[4096,256]{1,0:T(8,128)(2,1)S(1)}, bf16[4096,256]{1,0:T(8,128)(2,1)S(1)}) fusion(f32[256]{0:T(256)S(1)} %get-tuple-element.336, f32[4096]{0:T(1024)S(1)} %get-tuple-element.337, f32[256]{0:T(256)S(1)} %get-tuple-element.334, f32[4096]{0:T(1024)S(1)} %get-tuple-element.335, f32[256]{0:T(256)S(1)} %get-tuple-element.338, f32[]{:T(128)S(6)} %mul.373), kind=kLoop, calls=%fused_computation.10.clone.1 | loop fusion | flops 8388608 | bytes 4230148 | tf_op jit(solution)/shard_map/convert
  592.2 6.4 %all-reduce.1 = f32[4,256]{1,0:T(4,128)S(1)} all-reduce(f32[4,256]{1,0:T(4,128)S(1)} %broadcast_multiply_fusion), channel_id=2, replica_groups=mesh['sector'=128,'blk'=2] {'blk'}, use_global_device_ids=true, to_apply=%region_3.4.clone | all-reduce | flops 1024 | bytes 8192
  (185 shorter events, 117.7 us)
Async XLA Ops:
  0.0 239.6 %copy-start = (f32[2,8192]{1,0:T(2,128)S(1)}, f32[2,8192]{1,0:T(2,128)}, u32[]{:S(2)}) copy-start(f32[2,8192]{1,0:T(2,128)} %param.9) | copy-start | bytes 196612
  0.0 15.0 %collective-permute-start = (bf16[2,32,8192]{2,1,0:T(8,128)(2,1)}, bf16[2,32,8192]{2,1,0:T(8,128)(2,1)S(1)}, u32[]{:S(2)}, u32[]{:S(2)}) collective-permute-start(bf16[2,32,8192]{2,1,0:T(8,128)(2,1)} %param.7), channel_id=1, source_target_pairs={{0,254},{2,0},{4,2},{6,4},{8,6},{10,8},{12,10},{14,12},{16,14},{18... | collective-permute-start | bytes 3145736 | tf_op jit(solution)/shard_map/ppermute | solution.py:14
  16.5 24.4 %collective-permute-start.1 = (bf16[2,32,8192]{2,1,0:T(8,128)(2,1)S(1)}, bf16[2,32,8192]{2,1,0:T(8,128)(2,1)S(1)}, u32[]{:S(2)}, u32[]{:S(2)}) collective-permute-start(bf16[2,32,8192]{2,1,0:T(8,128)(2,1)S(1)} %broadcast_select_fusion), channel_id=1, source_target_pairs={{0,252},{2,254},{4,0},{6,2},{8,4},{10,6},{12,8},{14,10},{16,12},{1... | collective-permute-start | bytes 3145736 | tf_op jit(solution)/shard_map/ppermute | solution.py:14
  41.1 26.8 %collective-permute-start.2 = (bf16[2,32,8192]{2,1,0:T(8,128)(2,1)S(1)}, bf16[2,32,8192]{2,1,0:T(8,128)(2,1)S(1)}, u32[]{:S(2)}, u32[]{:S(2)}) collective-permute-start(bf16[2,32,8192]{2,1,0:T(8,128)(2,1)S(1)} %broadcast_select_fusion.1), channel_id=1, source_target_pairs={{0,248},{2,250},{4,252},{6,254},{8,0},{10,2},{12,4},{14,6},{16,8},... | collective-permute-start | bytes 3145736 | tf_op jit(solution)/shard_map/ppermute | solution.py:14
  68.0 25.3 %collective-permute-start.3 = (bf16[2,32,8192]{2,1,0:T(8,128)(2,1)S(1)}, bf16[2,32,8192]{2,1,0:T(8,128)(2,1)S(1)}, u32[]{:S(2)}, u32[]{:S(2)}) collective-permute-start(bf16[2,32,8192]{2,1,0:T(8,128)(2,1)S(1)} %broadcast_select_fusion.2), channel_id=1, source_target_pairs={{0,240},{2,242},{4,244},{6,246},{8,248},{10,250},{12,252},{14,254}... | collective-permute-start | bytes 3145736 | tf_op jit(solution)/shard_map/ppermute | solution.py:14
  93.5 28.2 %collective-permute-start.4 = (bf16[2,32,8192]{2,1,0:T(8,128)(2,1)S(1)}, bf16[2,32,8192]{2,1,0:T(8,128)(2,1)S(1)}, u32[]{:S(2)}, u32[]{:S(2)}) collective-permute-start(bf16[2,32,8192]{2,1,0:T(8,128)(2,1)S(1)} %broadcast_select_fusion.3), channel_id=1, source_target_pairs={{0,224},{2,226},{4,228},{6,230},{8,232},{10,234},{12,236},{14,238}... | collective-permute-start | bytes 3145736 | tf_op jit(solution)/shard_map/ppermute | solution.py:14
  121.9 32.4 %collective-permute-start.5 = (bf16[2,32,8192]{2,1,0:T(8,128)(2,1)S(1)}, bf16[2,32,8192]{2,1,0:T(8,128)(2,1)S(1)}, u32[]{:S(2)}, u32[]{:S(2)}) collective-permute-start(bf16[2,32,8192]{2,1,0:T(8,128)(2,1)S(1)} %broadcast_select_fusion.4), channel_id=1, source_target_pairs={{0,192},{2,194},{4,196},{6,198},{8,200},{10,202},{12,204},{14,206}... | collective-permute-start | bytes 3145736 | tf_op jit(solution)/shard_map/ppermute | solution.py:14
  154.4 48.4 %collective-permute-start.6 = (bf16[2,32,8192]{2,1,0:T(8,128)(2,1)S(1)}, bf16[2,32,8192]{2,1,0:T(8,128)(2,1)S(1)}, u32[]{:S(2)}, u32[]{:S(2)}) collective-permute-start(bf16[2,32,8192]{2,1,0:T(8,128)(2,1)S(1)} %broadcast_select_fusion.5), channel_id=1, source_target_pairs={{0,128},{2,130},{4,132},{6,134},{8,136},{10,138},{12,140},{14,142}... | collective-permute-start | bytes 3145736 | tf_op jit(solution)/shard_map/ppermute | solution.py:14
  202.9 28.9 %collective-permute-start.7 = (bf16[2,32,8192]{2,1,0:T(8,128)(2,1)S(1)}, bf16[2,32,8192]{2,1,0:T(8,128)(2,1)}, u32[]{:S(2)}, u32[]{:S(2)}) collective-permute-start(bf16[2,32,8192]{2,1,0:T(8,128)(2,1)S(1)} %broadcast_select_fusion.6), channel_id=1, source_target_pairs={{0,254},{2,0},{4,2},{6,4},{8,6},{10,8},{12,10},{14,12},{16,14},{18... | collective-permute-start | bytes 3145736 | tf_op jit(solution)/shard_map/ppermute | solution.py:14
  338.2 76.0 %copy-start.3 = (u32[256]{0:T(256)S(1)}, u32[256]{0:T(256)}, u32[]{:S(2)}) copy-start(u32[256]{0:T(256)} %constant.255) | copy-start | bytes 3076
  338.2 77.4 %copy-start.1 = (f32[256]{0:T(256)S(1)}, f32[256]{0:T(256)}, u32[]{:S(2)}) copy-start(f32[256]{0:T(256)} %param.10) | copy-start | bytes 3076
  338.2 77.5 %copy-start.2 = (f32[256]{0:T(256)S(1)}, f32[256]{0:T(256)}, u32[]{:S(2)}) copy-start(f32[256]{0:T(256)} %param.11) | copy-start | bytes 3076
  391.9 71.1 %all-to-all-start = ((bf16[128,2,3840]{2,1,0:T(2,128)(2,1)}), bf16[128,2,3840]{2,1,0:T(2,128)(2,1)S(1)}, u32[]{:S(2)}, u32[]{:S(2)}) async-start(bf16[128,2,3840]{2,1,0:T(2,128)(2,1)} %reshape.176), calls=%async_computation | async-start | bytes 3932160 | tf_op jit(solution)/shard_map/all_to_all | solution.py:109
